TPU v7x, 32 devices: a whole 2x2x4 slice. The times are simulated.
32 devices in a mesh: tgt: 8 (over z, core), sup: 4 (over y, x).
Axes of the slice: x: 2, y: 2, z: 4, core: 2. Of those that a mesh axis runs over, the one named last changes fastest.
Arguments:
- target_pool: float32 [512, 3, 1024], P('tgt'), may hold values from -6 to 6
- target_index: int32 [64], P('tgt'), may hold values from 0 to 511, as said below
- target_labels: int32 [64], P('tgt'), may hold values from 0 to 99
- dual_weights: float32 [128, 100], P('sup'), may hold values from -0.5 to 0.5
- support_images: float32 [128, 3, 1024], P(('sup', 'tgt')), may hold values from -6 to 6
Outputs:
- residual: float32 [64, 100], P('tgt')
- support_grad: float32 [128, 3, 1024], P(('sup', 'tgt'))
Inputs may be any that keep to these rules, and one draw needn't show every extreme that they name: `target_index`: for each j, the targets 8 * j to 8 * (j + 1) - 1 name distinct candidates among 64 * j to 64 * (j + 1) - 1.
All inputs are finite; a program needn't handle non-finite values.
Results may differ from a plain program's by a relative error of at most 0.0003.
Values sent between devices are 32-bit elements; how exact they have to be, the bound alone decides.
A program may use at most 64 MiB of HBM per device.

v0:
```python
import math

import jax
import jax.numpy as jnp
from jax import lax
from jax.sharding import PartitionSpec as P

CHANNELS = 3
SIDE = 32
CLASSES = 100
LAYERS = 3
PIXELS = 1024


bias_variance = 0.01


def box_filter(pixel_map):
    column = jnp.arange(PIXELS) % SIDE
    zero_column = jnp.zeros(pixel_map.shape[:-1] + (1,), pixel_map.dtype)
    shifted_right = jnp.concatenate([zero_column, pixel_map[..., :-1]], axis=-1)
    shifted_left = jnp.concatenate([pixel_map[..., 1:], zero_column], axis=-1)
    across = (
        pixel_map
        + jnp.where(column > 0, shifted_right, 0.0)
        + jnp.where(column < SIDE - 1, shifted_left, 0.0)
    )
    zero_row = jnp.zeros(pixel_map.shape[:-1] + (SIDE,), pixel_map.dtype)
    shifted_down = jnp.concatenate([zero_row, across[..., :-SIDE]], axis=-1)
    shifted_up = jnp.concatenate([across[..., SIDE:], zero_row], axis=-1)
    return (across + shifted_down + shifted_up) / 9.0


def self_maps(images):
    energy = images[:, 0] * images[:, 0]
    for channel in range(1, CHANNELS):
        energy = energy + images[:, channel] * images[:, channel]
    current = box_filter(energy / CHANNELS) + bias_variance
    levels = [current]
    for layer_index in range(1, LAYERS):
        current = box_filter(current) + bias_variance
        levels.append(current)
    return levels


def rectified(cross, target_level, support_level):
    spread = jnp.sqrt(target_level * support_level - cross * cross)
    polar_angle = jnp.arctan2(spread, cross)
    return ((spread + (math.pi - polar_angle) * cross) / math.pi, spread, polar_angle)


def cross_forward(targets, support, target_levels, support_levels):
    inner_sum = targets[:, None, 0] * support[None, :, 0]
    for channel in range(1, CHANNELS):
        inner_sum = inner_sum + targets[:, None, channel] * support[None, :, channel]
    cross = box_filter(inner_sum / CHANNELS) + bias_variance
    saved_maps = []
    output_map = cross
    for layer_index in range(LAYERS):
        output_map, spread, polar_angle = rectified(
            cross, target_levels[layer_index][:, None], support_levels[layer_index][None]
        )
        saved_maps.append((spread, polar_angle))
        if layer_index + 1 < LAYERS:
            cross = box_filter(output_map) + bias_variance
    return (jnp.mean(output_map, axis=-1), saved_maps)


def cross_backward(weight, saved_maps, targets, support, support_levels):
    upstream = weight[:, :, None]
    level_grad = None
    for layer_index in range(LAYERS - 1, -1, -1):
        spread, polar_angle = saved_maps[layer_index]
        level_term = jnp.sum(upstream * spread, axis=0) / (
            2.0 * math.pi * support_levels[layer_index]
        )
        level_grad = level_term if level_grad is None else level_term + box_filter(level_grad)
        upstream = box_filter(upstream * (math.pi - polar_angle) / math.pi)
    energy_grad = box_filter(level_grad) / CHANNELS
    channel_grads = []
    for channel in range(CHANNELS):
        carried = jnp.sum(upstream * targets[:, None, channel], axis=0) / CHANNELS
        channel_grads.append(carried + 2.0 * support[:, channel] * energy_grad)
    return jnp.stack(channel_grads, axis=1)


def shards(target_pool, target_index, target_labels, dual_weights, support_images):
    local_rows = target_index - lax.axis_index("tgt") * target_pool.shape[0]
    targets = jnp.take(target_pool, local_rows, axis=0)
    onehot = (target_labels[:, None] == jnp.arange(CLASSES)[None, :]).astype(jnp.float32)
    own_count = support_images.shape[0]
    all_targets, all_onehot = (
        lax.all_gather(targets, "tgt", axis=0, tiled=True),
        lax.all_gather(onehot, "tgt", axis=0, tiled=True),
    )
    own_duals = lax.dynamic_slice_in_dim(
        dual_weights, lax.axis_index("tgt") * own_count, own_count, 0
    )
    support_levels = self_maps(support_images)
    kernel, saved_maps = cross_forward(
        all_targets, support_images, self_maps(all_targets), support_levels
    )
    partial_value = jnp.dot(
        kernel, own_duals, precision=lax.Precision.HIGHEST, preferred_element_type=jnp.float32
    )
    predicted = lax.psum(partial_value, ("tgt", "sup"))
    residual_all = predicted - all_onehot
    weight = jnp.dot(
        residual_all,
        own_duals.T,
        precision=lax.Precision.HIGHEST,
        preferred_element_type=jnp.float32,
    )
    support_grad = cross_backward(weight, saved_maps, all_targets, support_images, support_levels)
    residual = lax.dynamic_slice_in_dim(
        residual_all, lax.axis_index("tgt") * targets.shape[0], targets.shape[0], 0
    )
    return (residual, support_grad)


def solution(mesh):
    in_specs = (
        P("tgt", None, None),
        P("tgt"),
        P("tgt"),
        P("sup", None),
        P(("sup", "tgt"), None, None),
    )
    out_specs = (P("tgt", None), P(("sup", "tgt"), None, None))
    return jax.shard_map(shards, mesh=mesh, in_specs=in_specs, out_specs=out_specs, check_vma=False)
```

profile of v0, /device:TPU:0, one launch (start us, length us, event | category | flops | bytes accessed | tf_op | source)
XLA Modules:
  0.0 109.1 jit_solution(5623943175997622236)
XLA Ops:
  0.7 0.7 copy-done.9
  1.8 0.7 gather_fusion
  2.6 17.2 %all_gather.6 = f32[64,3,1024]{2,0,1:T(8,128)S(1)} all-gather(f32[8,3,1024]{2,0,1:T(8,128)S(1)} %broadcast_select_fusion), channel_id=1, replica_groups=mesh['tgt'=8,'sup'=4] {'tgt'}, dimensions={0}, use_global_device_ids=true | all-gather | bytes 884736 | tf_op jit(solution)/shard_map/all_gather | solution.py:93
  19.8 0.9 broadcast_multiply_fusion.1
  21.3 0.7 copy-done.6
  22.3 0.4 fusion.26
  22.7 0.5 select_add_fusion.5
  23.9 2.3 %add_multiply_fusion.3 = (f32[64,4,1024]{2,0,1:T(8,128)S(1)}, f32[64,4,1024]{2,0,1:T(8,128)S(1)}) fusion(f32[4,1024]{1,0:T(4,128)S(1)} %multiply_add_fusion.10, f32[64,1024]{1,0:T(8,128)S(1)} %multiply_add_fusion.5, f32[64,4,992]{2,0,1:T(8,128)S(1)} %get-tuple-element.42, f32[64,4,1024]{2,0,1:T(8,128)S(1)} %select_add_fusion.5, ...), kind=kLoop, calls=%fused_computation.26 | loop fusion | flops 2883584 | bytes 5455872 | tf_op jit(solution)/shard_map/div | solution.py:49
  26.2 0.4 fusion.24
  26.6 0.5 select_add_fusion.4
  28.3 3.2 %add_multiply_fusion.2 = (f32[64,4,1024]{2,0,1:T(8,128)S(1)}, f32[64,4,1024]{2,0,1:T(8,128)}) fusion(f32[4,1024]{1,0:T(4,128)S(1)} %multiply_add_fusion.9, f32[64,1024]{1,0:T(8,128)S(1)} %multiply_add_fusion.4, f32[64,4,992]{2,0,1:T(8,128)S(1)} %get-tuple-element.38, f32[64,4,1024]{2,0,1:T(8,128)S(1)} %select_add_fusion.4, ...), kind=kLoop, calls=%fused_computation.21 | loop fusion | flops 2883584 | bytes 5455872 | tf_op jit(solution)/shard_map/div | solution.py:49
  31.5 0.4 fusion.22
  31.9 0.4 select_add_fusion.3
  33.7 2.7 %multiply_reduce_fusion.6 = (f32[64,4]{0,1:T(4,128)S(1)}, f32[64,4,1024]{2,0,1:T(8,128)S(1)}) fusion(f32[4,1024]{1,0:T(4,128)S(1)} %multiply_add_fusion.8, f32[64,1024]{1,0:T(8,128)S(1)} %multiply_add_fusion.3, f32[64,4,992]{2,0,1:T(8,128)S(1)} %get-tuple-element.34, f32[64,4,1024]{2,0,1:T(8,128)S(1)} %select_add_fusion.3, ...), kind=kLoop, calls=%fused_computation.16 | loop fusion | flops 3145472 | bytes 4408320 | tf_op jit(solution)/shard_map/reduce_sum | solution.py:66
  36.4 0.9 fusion.6
  37.3 40.9 %psum.7 = f32[64,100]{1,0:T(8,128)} all-reduce(f32[64,100]{1,0:T(8,128)S(1)} %fusion.6), channel_id=1, replica_groups=mesh['tgt'=8,'sup'=4] {'tgt','sup'}, use_global_device_ids=true, to_apply=%region_1.2 | all-reduce | flops 6400 | bytes 51200 | tf_op jit(solution)/shard_map/psum | solution.py:106
  78.3 14.2 %all_gather.7 = f32[64,100]{1,0:T(8,128)S(1)} all-gather(f32[8,100]{1,0:T(8,128)S(1)} %fusion.5), channel_id=1, replica_groups=mesh['tgt'=8,'sup'=4] {'tgt'}, dimensions={0}, use_global_device_ids=true | all-gather | bytes 28800 | tf_op jit(solution)/shard_map/all_gather | solution.py:94
  92.5 0.8 fusion.8
  93.4 3.1 %multiply_reduce_fusion.2 = (f32[4,1024]{1,0:T(4,128)S(1)}, f32[64,4,1024]{2,0,1:T(8,128)S(1)}) fusion(f32[64,4,1024]{2,0,1:T(8,128)S(1)} %get-tuple-element.8, f32[64,4]{0,1:T(4,128)S(1)} %fusion.8, f32[4,1024]{1,0:T(4,128)S(1)} %multiply_add_fusion.8, f32[64,1024]{1,0:T(8,128)} %copy-done.2), kind=kLoop, calls=%fused_computation.3 | loop fusion | flops 2093056 | bytes 2393088 | tf_op jit(solution)/shard_map/reduce_sum | solution.py:74
  96.7 0.4 fusion.20
  97.1 0.4 select_add_fusion.2
  97.9 0.8 copy-done.1
  98.7 2.3 %multiply_reduce_fusion.3 = (f32[4,1024]{1,0:T(4,128)S(1)}, f32[64,4,1024]{2,0,1:T(8,128)S(1)}) fusion(f32[64,4,1024]{2,0,1:T(8,128)S(1)} %copy-done.1, f32[4,1024]{1,0:T(4,128)S(1)} %multiply_add_fusion.9, f32[64,1024]{1,0:T(8,128)S(1)} %multiply_add_fusion.4, f32[64,4,992]{2,0,1:T(8,128)S(1)} %get-tuple-element.30, f32[64,4,1024]{2,0,1:T(8,128)S(1)} %select_add_fusion.2, ...), kind=kLoop, calls=%fused_computation.4 | loop fusion | flops 2879488 | bytes 5472256 | tf_op jit(solution)/shard_map/reduce_sum | solution.py:74
  101.4 0.4 fusion.18
  101.8 0.4 select_add_fusion.1
  102.6 2.3 %multiply_reduce_fusion.4 = (f32[4,1024]{1,0:T(4,128)S(1)}, f32[64,4,1024]{2,0,1:T(8,128)S(1)}) fusion(f32[64,4,1024]{2,0,1:T(8,128)S(1)} %get-tuple-element.12, f32[4,1024]{1,0:T(4,128)S(1)} %multiply_add_fusion.10, f32[64,1024]{1,0:T(8,128)S(1)} %multiply_add_fusion.5, f32[64,4,992]{2,0,1:T(8,128)S(1)} %get-tuple-element.26, ...), kind=kLoop, calls=%fused_computation.5 | loop fusion | flops 2879488 | bytes 5472256 | tf_op jit(solution)/shard_map/reduce_sum | solution.py:74
  105.2 0.4 fusion.16
  105.6 0.4 select_add_fusion
  106.5 0.5 copy-done.3
  107.2 0.5 multiply_reduce_fusion.5
  107.9 0.6 pad_maximum_fusion
  108.5 0.6 constant_dynamic-slice_fusion
  (70 shorter events, 6.9 us)
Async XLA Ops:
  0.6 1.2 %copy-start = (f32[64,3,1024]{2,0,1:T(8,128)S(1)}, f32[64,3,1024]{2,0,1:T(8,128)}, u32[]{:S(2)}) copy-start(f32[64,3,1024]{2,0,1:T(8,128)} %param.5) | copy-start | bytes 2359300
  0.7 0.7 copy-start.9
  21.3 0.8 copy-start.6
  33.4 3.0 %copy-start.2 = (f32[64,1024]{1,0:T(8,128)}, f32[64,1024]{1,0:T(8,128)S(1)}, u32[]{:S(2)}) copy-start(f32[64,1024]{1,0:T(8,128)S(1)} %multiply_add_fusion.3) | copy-start | bytes 786436
  37.3 40.9 %copy-start.8 = (s32[8]{0:T(128)S(1)}, s32[8]{0:T(128)}, u32[]{:S(2)}) copy-start(s32[8]{0:T(128)} %param.7) | copy-start | bytes 100
  78.2 14.3 %copy-start.7 = (f32[64,100]{1,0:T(8,128)S(1)}, f32[64,100]{1,0:T(8,128)}, u32[]{:S(2)}) copy-start(f32[64,100]{1,0:T(8,128)} %psum.7) | copy-start | bytes 76804
  97.5 1.2 %copy-start.1 = (f32[64,4,1024]{2,0,1:T(8,128)S(1)}, f32[64,4,1024]{2,0,1:T(8,128)}, u32[]{:S(2)}) copy-start(f32[64,4,1024]{2,0,1:T(8,128)} %get-tuple-element.10) | copy-start | bytes 3145732
  106.1 1.0 copy-start.3
  106.1 1.0 copy-start.4
  106.1 1.1 %copy-start.5 = (f32[64,1024]{1,0:T(8,128)S(1)}, f32[64,1024]{1,0:T(8,128)}, u32[]{:S(2)}) copy-start(f32[64,1024]{1,0:T(8,128)} %get-tuple-element.48) | copy-start | bytes 786436
where the time goes:
time: 110 us; the launch traced here: 109 us
  blocking collectives  72.3 us (66%)
  other arithmetic  22.9 us (21%)
  local copies, waits for them, and re-layouts  11.1 us (10%)
  matrix products  1.75 us (2%)
    psum x1, blocking collectives, shards(): predicted = lax.psum(partial_value, ('tgt', 'sup'))  40.9 us
    all_gather x1, blocking collectives, shards(): lax.all_gather(targets, 'tgt', axis=0, tiled=True)  17.2 us
    all_gather x1, blocking collectives, shards(): lax.all_gather(onehot, 'tgt', axis=0, tiled=True)  14.2 us
    reduce_sum x3, other arithmetic, cross_backward(): jnp.sum(upstream * spread, axis=0)  7.66 us
    div x2, other arithmetic, rectified(): (spread + (math.pi - polar_angle) * cross) / math.pi  5.48 us
    add x15, other arithmetic, box_filter(): pixel_map + jnp.where(column > 0, shifted_right, 0.0)  3.66 us
    unnamed x20, local copies, waits for them, and re-layouts  3.37 us
    slice x15, local copies, waits for them, and re-layouts, box_filter(): shifted_right = jnp.concatenate([zero_column, pixel_map[..., :-1]], axis=-1)  3.19 us

commit v1 on v0

v1 whole, which is shorter than its diff:
```python
import functools
import math

import jax
import jax.numpy as jnp
from jax import lax
from jax.experimental import pallas as pl
from jax.experimental.pallas import tpu as pltpu
from jax.sharding import PartitionSpec as P

CHANNELS = 3
SIDE = 32
CLASSES = 100
LAYERS = 3
PIXELS = 1024
BETA = 0.01
PACK = 4
SUB = 8
LANES = 128
MESH = pl.DeviceIdType.MESH
HIGH = lax.Precision.HIGHEST
ACOS = (
    1.5707963050,
    -0.2145988016,
    0.0889789874,
    -0.0501743046,
    0.0308918810,
    -0.0170881256,
    0.0066700901,
    -0.0012624911,
)


def masks():
    lane = lax.broadcasted_iota(jnp.int32, (SUB, LANES), 1)
    row = lax.broadcasted_iota(jnp.int32, (SUB, LANES), 0)
    column = lane % SIDE
    return (column > 0, column < SIDE - 1, row > 0, row < SUB - 1, lane // SIDE)


def box_sum(maps, mask):
    right, left, down, up, _ = mask
    axis = maps[0].ndim - 1

    def across(v):
        return (
            v
            + jnp.where(right, pltpu.roll(v, 1, axis), 0.0)
            + jnp.where(left, pltpu.roll(v, LANES - 1, axis), 0.0)
        )

    before = jnp.where(down, pltpu.roll(maps[3], 1, axis - 1), 0.0)
    after = jnp.where(up, pltpu.roll(maps[0], SUB - 1, axis - 1), 0.0)
    low = maps[0] + maps[1]
    high = maps[2] + maps[3]
    return [across(v) for v in (before + low, low + maps[2], maps[1] + high, high + after)]


def interleave(images, mask):
    group = mask[4]
    out = []
    for k in range(PACK):
        total = None
        for m in range(PACK):
            shift = ((m - k) * SIDE) % LANES
            moved = images[m] if shift == 0 else pltpu.roll(images[m], shift, 1)
            total = moved if total is None else jnp.where(group == m, moved, total)
        out.append(total)
    return out


def replicate(image, mask):
    group = mask[4]
    out = []
    rolled = [image] + [pltpu.roll(image, SIDE * s, 1) for s in range(1, PACK)]
    for k in range(PACK):
        total = None
        for m in range(PACK):
            moved = rolled[(m - k) % PACK]
            total = moved if total is None else jnp.where(group == m, moved, total)
        out.append(total)
    return out


def levels_of(images, mask):
    energy = []
    for k in range(PACK):
        total = images[0][k] * images[0][k]
        for channel in range(1, CHANNELS):
            total = total + images[channel][k] * images[channel][k]
        energy.append(total * (1.0 / CHANNELS))
    levels = []
    current = energy
    for _ in range(LAYERS):
        current = [v * (1.0 / 9.0) + BETA for v in box_sum(current, mask)]
        levels.append(current)
    return levels


def kernel(
    nt, ns, own_t, own_s,
    index_ref, label_ref, pool_ref, dual_ref, support_ref,
    residual_ref, grad_ref,
    tbuf, dbuf, kbuf, srep, sroot, tlev, amp, ang, ksum, wexp, accl, accc, pred, flat,
    plane_send, plane_recv, part_send, part_recv, dual_send, dual_recv, k_send, k_recv,
):
    ti = lax.axis_index("tgt")
    si = lax.axis_index("sup")
    chips = nt // 2
    chip = ti // 2
    core = ti % 2
    ndev = nt * ns
    me = si * nt + ti
    groups_own = own_t // PACK
    groups = nt * groups_own
    images = groups_own * CHANNELS * PACK
    targets = nt * own_t
    mask = masks()

    barrier = pltpu.get_barrier_semaphore()

    def greet(step, carry):
        other = lax.rem(me + step, ndev)
        pl.semaphore_signal(
            barrier, inc=1, device_id=(lax.rem(other, nt), other // nt), device_id_type=MESH
        )
        return carry

    lax.fori_loop(1, ndev, greet, 0)

    pool = pool_ref.shape[1] * SUB
    picks = [lax.rem(index_ref[t], pool) for t in range(own_t)]
    for gl in range(groups_own):
        for channel in range(CHANNELS):
            natural = [
                pool_ref[channel, at // SUB, :, pl.ds(at % SUB, 1), :].reshape(SUB, LANES)
                for at in picks[gl * PACK : (gl + 1) * PACK]
            ]
            phases = interleave(natural, mask)
            for k in range(PACK):
                tbuf[ti, (gl * CHANNELS + channel) * PACK + k] = phases[k]
    row = lax.broadcasted_iota(jnp.int32, (SUB, LANES), 0)
    lane = lax.broadcasted_iota(jnp.int32, (SUB, LANES), 1)
    label = jnp.zeros((SUB, LANES), jnp.int32)
    for r in range(own_t):
        label = jnp.where(row == r, label_ref[r], label)
    own_onehot = jnp.where(label == lane, 1.0, 0.0).astype(jnp.float32)
    tbuf[ti, images] = own_onehot
    dbuf[si] = dual_ref[...]

    pl.semaphore_wait(barrier, ndev - 1)

    def plane_copy(target_chip):
        return pltpu.make_async_remote_copy(
            src_ref=tbuf.at[ti],
            dst_ref=tbuf.at[ti],
            send_sem=plane_send.at[target_chip],
            recv_sem=plane_recv.at[chip],
            device_id=(target_chip * 2 + core, si),
            device_id_type=MESH,
        )

    def plane_arrival(source_chip):
        return pltpu.make_async_remote_copy(
            src_ref=tbuf.at[source_chip * 2 + core],
            dst_ref=tbuf.at[source_chip * 2 + core],
            send_sem=plane_send.at[source_chip],
            recv_sem=plane_recv.at[source_chip],
            device_id=(source_chip * 2 + core, si),
            device_id_type=MESH,
        )

    def part_copy(p):
        return pltpu.make_async_remote_copy(
            src_ref=tbuf.at[p * 2 + core],
            dst_ref=tbuf.at[p * 2 + core],
            send_sem=part_send.at[p],
            recv_sem=part_recv.at[p],
            device_id=(chip * 2 + 1 - core, si),
            device_id_type=MESH,
        )

    def part_arrival(p):
        return pltpu.make_async_remote_copy(
            src_ref=tbuf.at[p * 2 + 1 - core],
            dst_ref=tbuf.at[p * 2 + 1 - core],
            send_sem=part_send.at[p],
            recv_sem=part_recv.at[p],
            device_id=(chip * 2 + 1 - core, si),
            device_id_type=MESH,
        )

    def dual_copy(s):
        return pltpu.make_async_remote_copy(
            src_ref=dbuf.at[si],
            dst_ref=dbuf.at[si],
            send_sem=dual_send.at[s],
            recv_sem=dual_recv.at[si],
            device_id=(ti, s),
            device_id_type=MESH,
        )

    def dual_arrival(s):
        return pltpu.make_async_remote_copy(
            src_ref=dbuf.at[s],
            dst_ref=dbuf.at[s],
            send_sem=dual_send.at[s],
            recv_sem=dual_recv.at[s],
            device_id=(ti, s),
            device_id_type=MESH,
        )

    def k_copy(d):
        return pltpu.make_async_remote_copy(
            src_ref=kbuf.at[me],
            dst_ref=kbuf.at[me],
            send_sem=k_send.at[d],
            recv_sem=k_recv.at[me],
            device_id=(lax.rem(d, nt), d // nt),
            device_id_type=MESH,
        )

    def k_arrival(d):
        return pltpu.make_async_remote_copy(
            src_ref=kbuf.at[d],
            dst_ref=kbuf.at[d],
            send_sem=k_send.at[d],
            recv_sem=k_recv.at[d],
            device_id=(lax.rem(d, nt), d // nt),
            device_id_type=MESH,
        )

    for h in range(1, chips):
        @pl.when(chip >= h)
        def _():
            plane_copy(chip - h).start()

        @pl.when(chip + h < chips)
        def _():
            plane_copy(chip + h).start()

    def send_dual(step, carry):
        dual_copy(lax.rem(si + step, ns)).start()
        return carry

    lax.fori_loop(1, ns, send_dual, 0)

    for m in range(own_s):
        reps = []
        for channel in range(CHANNELS):
            phases = replicate(support_ref[channel, :, m, :], mask)
            reps.append(phases)
            for k in range(PACK):
                srep[channel, k, m] = phases[k]
        levels = levels_of(reps, mask)
        for layer in range(LAYERS):
            for k in range(PACK):
                inverse = lax.rsqrt(levels[layer][k])
                sroot[layer, 0, k, m] = inverse * (1.0 / 9.0**layer)
                sroot[layer, 1, k, m] = levels[layer][k] * inverse * (9.0**layer / math.pi)

    def group_forward(owner, gl):
        g = owner * groups_own + gl
        image = [
            [tbuf[owner, (gl * CHANNELS + channel) * PACK + k] for k in range(PACK)]
            for channel in range(CHANNELS)
        ]
        levels = levels_of(image, mask)
        for layer in range(LAYERS):
            for k in range(PACK):
                inverse = lax.rsqrt(levels[layer][k])
                tlev[layer, 0, k] = inverse
                tlev[layer, 1, k] = levels[layer][k] * inverse
        current = []
        for k in range(PACK):
            total = image[0][k][None] * srep[0, k]
            for channel in range(1, CHANNELS):
                total = total + image[channel][k][None] * srep[channel, k]
            current.append(total)
        cross = [v * (1.0 / 27.0) + BETA for v in box_sum(current, mask)]
        for layer in range(LAYERS):
            mapped = []
            for k in range(PACK):
                x = cross[k] * (tlev[layer, 0, k][None] * sroot[layer, 0, k])
                size = jnp.abs(x)
                gap = jnp.maximum(1.0 - size, 1e-20)
                rest = 1.0 + size
                half = gap * lax.rsqrt(gap)
                poly = size * (ACOS[7] / math.pi) + ACOS[6] / math.pi
                for term in ACOS[5::-1]:
                    poly = poly * size + term / math.pi
                near = half * poly
                slope = jnp.where(x >= 0.0, 1.0 - near, near)
                sine = half * (rest * lax.rsqrt(rest))
                scaled = sine * tlev[layer, 1, k][None]
                amp[g, layer, k] = scaled
                ang[g, layer, k] = slope
                mapped.append(scaled * sroot[layer, 1, k] + slope * cross[k])
            if layer + 1 < LAYERS:
                cross = [v + BETA * 9.0 ** (layer + 1) for v in box_sum(mapped, mask)]
        total = (mapped[0] + mapped[1]) + (mapped[2] + mapped[3])
        ksum[:, pl.ds(g, 1), :] = jnp.sum(total, axis=1, keepdims=True)

    def block_forward(owner):
        def one(gl, carry):
            group_forward(owner, gl)
            return carry

        lax.fori_loop(0, groups_own, one, 0)

    def order(n):
        both = jnp.minimum(chip, chips - 1 - chip)
        h = (n + 1) // 2
        two_sided = jnp.where(n % 2 == 1, chip - h, chip + h)
        far = n - both
        one_sided = jnp.where(chip <= chips - 1 - chip, chip + far, chip - far)
        return jnp.where(n <= 2 * both, two_sided, one_sided)

    def visit(n, carry):
        p = order(n)

        @pl.when(n > 0)
        def _():
            plane_arrival(p).wait_recv()

        part_copy(p).start()
        block_forward(p * 2 + core)
        part_arrival(p).wait_recv()
        block_forward(p * 2 + 1 - core)
        return carry

    lax.fori_loop(0, chips, visit, 0)

    spread_row = lax.broadcasted_iota(jnp.int32, (targets, LANES), 0)
    spread_lane = lax.broadcasted_iota(jnp.int32, (targets, LANES), 1)
    spread = jnp.where(spread_row % PACK == spread_lane // SIDE, 1.0, 0.0).astype(jnp.float32)
    keep_g = lax.broadcasted_iota(jnp.int32, (groups, targets), 0)
    keep_t = lax.broadcasted_iota(jnp.int32, (groups, targets), 1)
    keep = jnp.where(keep_t // PACK == keep_g, 1.0, 0.0).astype(jnp.float32)
    nt_dims = (((1,), (1,)), ((), ()))
    lane_sums = lax.dot_general(
        ksum[...].reshape(own_s * groups, LANES), spread, nt_dims,
        precision=HIGH, preferred_element_type=jnp.float32,
    ) * (1.0 / (PIXELS * 9.0 ** (LAYERS - 1)))
    picked = jnp.sum(lane_sums.reshape(own_s, groups, targets) * keep[None], axis=1)
    kbuf[me] = picked

    def send_k(step, carry):
        k_copy(lax.rem(me + step, ndev)).start()
        return carry

    lax.fori_loop(1, ndev, send_k, 0)

    def take_dual(step, carry):
        dual_arrival(lax.rem(si + step, ns)).wait_recv()
        return carry

    lax.fori_loop(1, ns, take_dual, 0)
    duals = dbuf[...].reshape(ns * dual_ref.shape[0], CLASSES)
    own_duals = dual_ref[pl.ds(ti * own_s, own_s), :]
    gram = lax.dot_general(
        own_duals, duals, nt_dims, precision=HIGH, preferred_element_type=jnp.float32
    )
    onehot = tbuf[:, images].reshape(targets, LANES)[:, :CLASSES]
    offset = lax.dot_general(
        own_duals, onehot, nt_dims, precision=HIGH, preferred_element_type=jnp.float32
    )
    accl[...] = jnp.zeros_like(accl)
    accc[...] = jnp.zeros_like(accc)

    def take_k(step, carry):
        k_arrival(lax.rem(me + step, ndev)).wait_recv()
        return carry

    lax.fori_loop(1, ndev, take_k, 0)
    columns = jnp.concatenate([kbuf[d] for d in range(ndev)], axis=0)
    weight = jnp.dot(gram, columns, precision=HIGH, preferred_element_type=jnp.float32) - offset
    wide = (weight[:, None, :] * keep[None]).reshape(own_s * groups, targets)
    wexp[...] = jnp.dot(
        wide, spread, precision=HIGH, preferred_element_type=jnp.float32
    ).reshape(own_s, groups, LANES)

    def block_backward(owner, carry):
        level_terms = [[None] * PACK for _ in range(LAYERS)]
        channel_terms = [[None] * PACK for _ in range(CHANNELS)]

        def add(table, at, k, value):
            table[at][k] = value if table[at][k] is None else table[at][k] + value

        for gl in range(groups_own):
            g = owner * groups_own + gl
            upstream = [jnp.broadcast_to(wexp[:, pl.ds(g, 1), :], (own_s, SUB, LANES))] * PACK
            for layer in range(LAYERS - 1, -1, -1):
                passed = []
                for k in range(PACK):
                    add(level_terms, layer, k, upstream[k] * amp[g, layer, k])
                    passed.append(upstream[k] * ang[g, layer, k])
                upstream = box_sum(passed, mask)
            for channel in range(CHANNELS):
                for k in range(PACK):
                    image = tbuf[owner, (gl * CHANNELS + channel) * PACK + k]
                    add(channel_terms, channel, k, upstream[k] * image[None])
        for layer in range(LAYERS):
            for k in range(PACK):
                accl[layer, k] += level_terms[layer][k]
        for channel in range(CHANNELS):
            for k in range(PACK):
                accc[channel, k] += channel_terms[channel][k]
        return carry

    lax.fori_loop(0, nt, block_backward, 0)

    def over_images(v):
        v = v + pltpu.roll(v, 2 * SIDE, 2)
        return v + pltpu.roll(v, SIDE, 2)

    level_grad = None
    for layer in range(LAYERS - 1, -1, -1):
        scale = 9.0**layer / (2.0 * math.pi * 9.0 ** (LAYERS - 1 - layer))
        term = [
            over_images(accl[layer, k]) * (sroot[layer, 0, k] * scale) for k in range(PACK)
        ]
        if level_grad is not None:
            carried = box_sum(level_grad, mask)
            term = [t + c * (1.0 / 9.0) for t, c in zip(term, carried)]
        level_grad = term
    energy = [v * (2.0 / (9.0 * CHANNELS)) for v in box_sum(level_grad, mask)]
    for channel in range(CHANNELS):
        natural = None
        for k in range(PACK):
            value = over_images(accc[channel, k]) * (1.0 / (CHANNELS * 9.0**LAYERS))
            value = value + srep[channel, k] * energy[k]
            natural = value if natural is None else jnp.where(mask[4] == k, value, natural)
        flat[...] = natural
        for s in range(SUB):
            grad_ref[channel, s] = flat[:, s, :]

    pred[...] = jnp.dot(columns.T, duals, precision=HIGH, preferred_element_type=jnp.float32)
    residual_ref[...] = pred[pl.ds(ti * own_t, own_t), :] - own_onehot[:own_t, :CLASSES]

    for p in range(chips):
        @pl.when(chip != p)
        def _():
            plane_copy(p).wait_send()

        part_copy(p).wait_send()

    def drain_dual(step, carry):
        dual_copy(lax.rem(si + step, ns)).wait_send()
        return carry

    lax.fori_loop(1, ns, drain_dual, 0)

    def drain_k(step, carry):
        k_copy(lax.rem(me + step, ndev)).wait_send()
        return carry

    lax.fori_loop(1, ndev, drain_k, 0)


def shards(nt, ns, target_pool, target_index, target_labels, dual_weights, support_images):
    own_t = target_index.shape[0]
    own_s = support_images.shape[0]
    groups = nt * own_t // PACK
    images = own_t * CHANNELS
    chips = nt // 2
    ndev = nt * ns
    f32 = jnp.float32
    vmem = pl.BlockSpec(memory_space=pltpu.VMEM)
    smem = pl.BlockSpec(memory_space=pltpu.SMEM)
    dma = pltpu.SemaphoreType.DMA
    tile = (SUB, LANES)
    residual, grad = pl.pallas_call(
        functools.partial(kernel, nt, ns, own_t, own_s),
        out_shape=(
            jax.ShapeDtypeStruct((own_t, CLASSES), f32),
            jax.ShapeDtypeStruct((CHANNELS, SUB, own_s, LANES), f32),
        ),
        in_specs=[smem, smem, vmem, vmem, vmem],
        out_specs=(vmem, vmem),
        scratch_shapes=[
            pltpu.VMEM((nt, images + 1) + tile, f32),
            pltpu.VMEM((ns,) + dual_weights.shape, f32),
            pltpu.VMEM((ndev, own_s, nt * own_t), f32),
            pltpu.VMEM((CHANNELS, PACK, own_s) + tile, f32),
            pltpu.VMEM((LAYERS, 2, PACK, own_s) + tile, f32),
            pltpu.VMEM((LAYERS, 2, PACK) + tile, f32),
            pltpu.VMEM((groups, LAYERS, PACK, own_s) + tile, f32),
            pltpu.VMEM((groups, LAYERS, PACK, own_s) + tile, f32),
            pltpu.VMEM((own_s, groups, LANES), f32),
            pltpu.VMEM((own_s, groups, LANES), f32),
            pltpu.VMEM((LAYERS, PACK, own_s) + tile, f32),
            pltpu.VMEM((CHANNELS, PACK, own_s) + tile, f32),
            pltpu.VMEM((nt * own_t, CLASSES), f32),
            pltpu.VMEM((own_s,) + tile, f32),
            dma((chips,)),
            dma((chips,)),
            dma((chips,)),
            dma((chips,)),
            dma((ns,)),
            dma((ns,)),
            dma((ndev,)),
            dma((ndev,)),
        ],
        compiler_params=pltpu.CompilerParams(collective_id=0, has_side_effects=True),
    )(
        target_index,
        target_labels,
        target_pool.reshape(-1, SUB, CHANNELS, SUB, LANES).transpose(2, 0, 3, 1, 4),
        dual_weights,
        support_images.reshape(own_s, CHANNELS, SUB, LANES).transpose(1, 2, 0, 3),
    )
    return (residual, grad.transpose(2, 0, 1, 3).reshape(support_images.shape))


def solution(mesh):
    in_specs = (
        P("tgt", None, None),
        P("tgt"),
        P("tgt"),
        P("sup", None),
        P(("sup", "tgt"), None, None),
    )
    out_specs = (P("tgt", None), P(("sup", "tgt"), None, None))
    body = functools.partial(shards, mesh.shape["tgt"], mesh.shape["sup"])
    return jax.shard_map(body, mesh=mesh, in_specs=in_specs, out_specs=out_specs, check_vma=False)
```

time: 110 us -> 38.1 us (0.35)
  blocking collectives: 72.3 us -> 0 us
  Pallas kernels: 0 us -> 34.6 us
  other arithmetic: 22.9 us -> 0 us
  local copies, waits for them, and re-layouts: 11.1 us -> 2.68 us
  matrix products: 1.75 us -> 0 us
    psum x1 -> x0, blocking collectives: 40.9 us -> none  [shards(): predicted = lax.psum(partial_value, ('tgt', 'sup'))]
    pallas_call x0 -> x1, Pallas kernels: none -> 34.6 us  [shards(): pl.pallas_call(functools.partial(kernel, nt, ns, own_t, own_s), out_shape...]
    all_gather x2 -> x0, blocking collectives: 31.4 us -> none  [the longest x1 17.2 us: shards(): lax.all_gather(targets, 'tgt', axis=0, tiled=True)]
    reduce_sum x5 -> x0, other arithmetic: 10.9 us -> none  [the longest x3 7.66 us: cross_backward(): jnp.sum(upstream * spread, axis=0)]
    slice x30 -> x0, local copies, waits for them, and re-layouts: 6.33 us -> none  [the longest x15 3.19 us: box_filter(): shifted_right = jnp.concatenate([zero_column, pixel_map[..., :-1]], axis=-1)]
    div x5 -> x0, other arithmetic: 5.71 us -> none  [the longest x2 5.48 us: rectified(): (spread + (math.pi - polar_angle) * cross) / math.pi]
    add x23 -> x0, other arithmetic: 4.51 us -> none  [the longest x15 3.66 us: box_filter(): pixel_map + jnp.where(column > 0, shifted_right, 0.0)]
    dot_general x2 -> x0, matrix products: 1.75 us -> none  [the longest x1 0.92 us: shards(): jnp.dot(kernel, own_duals, precision=lax.Precision.HIGHEST, preferred_ele...]
where the time goes in v1:
time: 38.1 us; the launch traced here: 37.9 us
  Pallas kernels  34.6 us (91%)
  local copies, waits for them, and re-layouts  2.68 us (7%)
  between operations  0.65 us (2%)
    pallas_call x1, Pallas kernels, shards(): pl.pallas_call(functools.partial(kernel, nt, ns, own_t, own_s), out_shape...  34.6 us
    unnamed x4, local copies, waits for them, and re-layouts  2.68 us

profile of v1, /device:TPU:0, one launch (start us, length us, event | category | flops | bytes accessed | tf_op | source)
XLA Modules:
  0.0 37.9 jit_solution(9450838641921274315)
XLA Ops:
  0.6 34.6 %shard_map.68 = (f32[8,100]{1,0:T(8,128)}, f32[3,8,4,128]{3,2,1,0:T(4,128)}) custom-call(s32[8]{0:T(128)} %index_ref.1, s32[8]{0:T(128)} %label_ref.1, f32[3,8,8,8,128]{4,3,2,1,0:T(8,128)} %bitcast.9, f32[32,100]{1,0:T(8,128)} %dual_ref.1, f32[3,8,4,128]{3,2,1,0:T(4,128)} %bitcast.11), custom_call_target="tpu_custom_call" | custom-call | tf_op jit(solution)/shard_map/pallas_call | solution.py:473
  35.2 0.0 copy-start
  35.2 0.7 %copy-done = f32[8,100]{1,0:T(8,128)S(1)} copy-done((f32[8,100]{1,0:T(8,128)S(1)}, f32[8,100]{1,0:T(8,128)}, u32[]{:S(2)}) %copy-start) | copy-done | bytes 3224
  35.9 0.6 %copy.9 = f32[8,100]{1,0:T(8,128)} copy(f32[8,100]{1,0:T(8,128)S(1)} %copy-done) | data formatting | bytes 6400
  36.5 1.4 %copy.10 = f32[4,3,1024]{2,0,1:T(4,128)} copy(f32[4,3,1024]{2,0,1:T(4,128)} %bitcast.10) | data formatting | bytes 98304
Async XLA Ops:
  35.2 0.7 %copy-start = (f32[8,100]{1,0:T(8,128)S(1)}, f32[8,100]{1,0:T(8,128)}, u32[]{:S(2)}) copy-start(f32[8,100]{1,0:T(8,128)} %get-tuple-element.8) | copy-start | bytes 9604

commit v2 on v1

--- a/solution.py
+++ b/solution.py
@@ -119,14 +119,15 @@
 
     barrier = pltpu.get_barrier_semaphore()
 
-    def greet(step, carry):
-        other = lax.rem(me + step, ndev)
-        pl.semaphore_signal(
-            barrier, inc=1, device_id=(lax.rem(other, nt), other // nt), device_id_type=MESH
-        )
-        return carry
-
-    lax.fori_loop(1, ndev, greet, 0)
+    def others(action):
+        for s in range(ns):
+            for t in range(nt):
+                pl.when((si != s) | (ti != t))(functools.partial(action, t, s))
+
+    def greet(t, s):
+        pl.semaphore_signal(barrier, inc=1, device_id=(t, s), device_id_type=MESH)
+
+    others(greet)
 
     pool = pool_ref.shape[1] * SUB
     picks = [lax.rem(index_ref[t], pool) for t in range(own_t)]
@@ -150,45 +151,48 @@
 
     pl.semaphore_wait(barrier, ndev - 1)
 
-    def plane_copy(target_chip):
+    def chunk(owner, gl):
+        first = gl * CHANNELS * PACK
+        last = images + 1 if gl == groups_own - 1 else first + CHANNELS * PACK
+        return tbuf.at[owner, pl.ds(first, last - first)]
+
+    def plane_copy(source_chip, gl, way, target_chip):
+        part = chunk(source_chip * 2 + core, gl)
         return pltpu.make_async_remote_copy(
-            src_ref=tbuf.at[ti],
-            dst_ref=tbuf.at[ti],
-            send_sem=plane_send.at[target_chip],
-            recv_sem=plane_recv.at[chip],
+            src_ref=part,
+            dst_ref=part,
+            send_sem=plane_send.at[way, source_chip, gl],
+            recv_sem=plane_recv.at[source_chip, gl],
             device_id=(target_chip * 2 + core, si),
             device_id_type=MESH,
         )
 
-    def plane_arrival(source_chip):
+    def part_copy(p, gl, side):
+        part = chunk(p * 2 + side, gl)
         return pltpu.make_async_remote_copy(
-            src_ref=tbuf.at[source_chip * 2 + core],
-            dst_ref=tbuf.at[source_chip * 2 + core],
-            send_sem=plane_send.at[source_chip],
-            recv_sem=plane_recv.at[source_chip],
-            device_id=(source_chip * 2 + core, si),
-            device_id_type=MESH,
-        )
-
-    def part_copy(p):
-        return pltpu.make_async_remote_copy(
-            src_ref=tbuf.at[p * 2 + core],
-            dst_ref=tbuf.at[p * 2 + core],
-            send_sem=part_send.at[p],
-            recv_sem=part_recv.at[p],
+            src_ref=part,
+            dst_ref=part,
+            send_sem=part_send.at[p, gl],
+            recv_sem=part_recv.at[p, gl],
             device_id=(chip * 2 + 1 - core, si),
             device_id_type=MESH,
         )
 
-    def part_arrival(p):
-        return pltpu.make_async_remote_copy(
-            src_ref=tbuf.at[p * 2 + 1 - core],
-            dst_ref=tbuf.at[p * 2 + 1 - core],
-            send_sem=part_send.at[p],
-            recv_sem=part_recv.at[p],
-            device_id=(chip * 2 + 1 - core, si),
-            device_id_type=MESH,
-        )
+    def handle(h, gl):
+        for way in range(2):
+            step = 1 - 2 * way
+            source = chip - step * h
+            onward = chip + step
+
+            @pl.when((source >= 0) & (source < chips))
+            def _():
+                plane_copy(source, gl, way, source).wait_recv()
+
+                @pl.when((onward >= 0) & (onward < chips))
+                def _():
+                    plane_copy(source, gl, way, onward).start()
+
+                part_copy(source, gl, core).start()
 
     def dual_copy(s):
         return pltpu.make_async_remote_copy(
@@ -210,34 +214,36 @@
             device_id_type=MESH,
         )
 
-    def k_copy(d):
+    def k_copy(t, s):
         return pltpu.make_async_remote_copy(
             src_ref=kbuf.at[me],
             dst_ref=kbuf.at[me],
-            send_sem=k_send.at[d],
-            recv_sem=k_recv.at[me],
-            device_id=(lax.rem(d, nt), d // nt),
+            send_sem=k_send,
+            recv_sem=k_recv,
+            device_id=(t, s),
             device_id_type=MESH,
         )
 
-    def k_arrival(d):
+    def k_all():
+        others_slots = kbuf.at[pl.ds(0, ndev - 1)]
         return pltpu.make_async_remote_copy(
-            src_ref=kbuf.at[d],
-            dst_ref=kbuf.at[d],
-            send_sem=k_send.at[d],
-            recv_sem=k_recv.at[d],
-            device_id=(lax.rem(d, nt), d // nt),
+            src_ref=others_slots,
+            dst_ref=others_slots,
+            send_sem=k_send,
+            recv_sem=k_recv,
+            device_id=(1 - core + chip * 2, si),
             device_id_type=MESH,
         )
 
-    for h in range(1, chips):
-        @pl.when(chip >= h)
-        def _():
-            plane_copy(chip - h).start()
-
-        @pl.when(chip + h < chips)
-        def _():
-            plane_copy(chip + h).start()
+    for gl in range(groups_own):
+        for way in range(2):
+            onward = chip + 1 - 2 * way
+
+            @pl.when((onward >= 0) & (onward < chips))
+            def _():
+                plane_copy(chip, gl, way, onward).start()
+
+        part_copy(chip, gl, core).start()
 
     def send_dual(step, carry):
         dual_copy(lax.rem(si + step, ns)).start()
@@ -301,13 +307,6 @@
         total = (mapped[0] + mapped[1]) + (mapped[2] + mapped[3])
         ksum[:, pl.ds(g, 1), :] = jnp.sum(total, axis=1, keepdims=True)
 
-    def block_forward(owner):
-        def one(gl, carry):
-            group_forward(owner, gl)
-            return carry
-
-        lax.fori_loop(0, groups_own, one, 0)
-
     def order(n):
         both = jnp.minimum(chip, chips - 1 - chip)
         h = (n + 1) // 2
@@ -316,20 +315,24 @@
         one_sided = jnp.where(chip <= chips - 1 - chip, chip + far, chip - far)
         return jnp.where(n <= 2 * both, two_sided, one_sided)
 
-    def visit(n, carry):
+    def visit(slot, carry):
+        n = slot // (2 * groups_own)
+        at = slot % (2 * groups_own)
+        gl = at % groups_own
         p = order(n)
-
-        @pl.when(n > 0)
-        def _():
-            plane_arrival(p).wait_recv()
-
-        part_copy(p).start()
-        block_forward(p * 2 + core)
-        part_arrival(p).wait_recv()
-        block_forward(p * 2 + 1 - core)
+        for later in range(1, groups_own):
+            pl.when((n > 0) & (at == later))(functools.partial(handle, n, later))
+        pl.when((n + 1 < chips) & (at == 2 * groups_own - 1))(functools.partial(handle, n + 1, 0))
+        for which in range(groups_own):
+            @pl.when(at == groups_own + which)
+            def _():
+                part_copy(p, which, 1 - core).wait_recv()
+
+        side = jnp.where(at < groups_own, core, 1 - core)
+        group_forward(p * 2 + side, gl)
         return carry
 
-    lax.fori_loop(0, chips, visit, 0)
+    lax.fori_loop(0, 2 * groups_own * chips, visit, 0)
 
     spread_row = lax.broadcasted_iota(jnp.int32, (targets, LANES), 0)
     spread_lane = lax.broadcasted_iota(jnp.int32, (targets, LANES), 1)
@@ -345,11 +348,7 @@
     picked = jnp.sum(lane_sums.reshape(own_s, groups, targets) * keep[None], axis=1)
     kbuf[me] = picked
 
-    def send_k(step, carry):
-        k_copy(lax.rem(me + step, ndev)).start()
-        return carry
-
-    lax.fori_loop(1, ndev, send_k, 0)
+    others(lambda t, s: k_copy(t, s).start())
 
     def take_dual(step, carry):
         dual_arrival(lax.rem(si + step, ns)).wait_recv()
@@ -368,11 +367,7 @@
     accl[...] = jnp.zeros_like(accl)
     accc[...] = jnp.zeros_like(accc)
 
-    def take_k(step, carry):
-        k_arrival(lax.rem(me + step, ndev)).wait_recv()
-        return carry
-
-    lax.fori_loop(1, ndev, take_k, 0)
+    k_all().wait_recv()
     columns = jnp.concatenate([kbuf[d] for d in range(ndev)], axis=0)
     weight = jnp.dot(gram, columns, precision=HIGH, preferred_element_type=jnp.float32) - offset
     wide = (weight[:, None, :] * keep[None]).reshape(own_s * groups, targets)
@@ -438,12 +433,18 @@
     pred[...] = jnp.dot(columns.T, duals, precision=HIGH, preferred_element_type=jnp.float32)
     residual_ref[...] = pred[pl.ds(ti * own_t, own_t), :] - own_onehot[:own_t, :CLASSES]
 
-    for p in range(chips):
-        @pl.when(chip != p)
-        def _():
-            plane_copy(p).wait_send()
-
-        part_copy(p).wait_send()
+    for gl in range(groups_own):
+        for way in range(2):
+            onward = chip + 1 - 2 * way
+            for h in range(chips):
+                source = chip - (1 - 2 * way) * h
+
+                @pl.when((source >= 0) & (source < chips) & (onward >= 0) & (onward < chips))
+                def _():
+                    plane_copy(source, gl, way, onward).wait_send()
+
+        for p in range(chips):
+            part_copy(p, gl, core).wait_send()
 
     def drain_dual(step, carry):
         dual_copy(lax.rem(si + step, ns)).wait_send()
@@ -451,11 +452,7 @@
 
     lax.fori_loop(1, ns, drain_dual, 0)
 
-    def drain_k(step, carry):
-        k_copy(lax.rem(me + step, ndev)).wait_send()
-        return carry
-
-    lax.fori_loop(1, ndev, drain_k, 0)
+    k_all().wait_send()
 
 
 def shards(nt, ns, target_pool, target_index, target_labels, dual_weights, support_images):
@@ -493,14 +490,14 @@
             pltpu.VMEM((CHANNELS, PACK, own_s) + tile, f32),
             pltpu.VMEM((nt * own_t, CLASSES), f32),
             pltpu.VMEM((own_s,) + tile, f32),
-            dma((chips,)),
-            dma((chips,)),
-            dma((chips,)),
-            dma((chips,)),
+            dma((2, chips, own_t // PACK)),
+            dma((chips, own_t // PACK)),
+            dma((chips, own_t // PACK)),
+            dma((chips, own_t // PACK)),
             dma((ns,)),
             dma((ns,)),
-            dma((ndev,)),
-            dma((ndev,)),
+            dma,
+            dma,
         ],
         compiler_params=pltpu.CompilerParams(collective_id=0, has_side_effects=True),
     )(

time: 38.1 us -> 34.4 us (0.903)
  Pallas kernels: 34.6 us -> 30.9 us
    pallas_call x1, Pallas kernels: 34.6 us -> 30.9 us  [shards(): pl.pallas_call(functools.partial(kernel, nt, ns, own_t, own_s), out_shape...]
where the time goes in v2:
time: 34.4 us; the launch traced here: 34.2 us
  Pallas kernels  30.9 us (90%)
  local copies, waits for them, and re-layouts  2.68 us (8%)
  between operations  0.65 us (2%)
    pallas_call x1, Pallas kernels, shards(): pl.pallas_call(functools.partial(kernel, nt, ns, own_t, own_s), out_shape...  30.9 us
    unnamed x4, local copies, waits for them, and re-layouts  2.68 us

profile of v2, /device:TPU:0, one launch (start us, length us, event | category | flops | bytes accessed | tf_op | source)
XLA Modules:
  0.0 34.2 jit_solution(1540620220992434535)
XLA Ops:
  0.6 30.9 %shard_map.68 = (f32[8,100]{1,0:T(8,128)}, f32[3,8,4,128]{3,2,1,0:T(4,128)}) custom-call(s32[8]{0:T(128)} %index_ref.1, s32[8]{0:T(128)} %label_ref.1, f32[3,8,8,8,128]{4,3,2,1,0:T(8,128)} %bitcast.9, f32[32,100]{1,0:T(8,128)} %dual_ref.1, f32[3,8,4,128]{3,2,1,0:T(4,128)} %bitcast.11), custom_call_target="tpu_custom_call" | custom-call | tf_op jit(solution)/shard_map/pallas_call | solution.py:470
  31.5 0.0 copy-start
  31.5 0.7 %copy-done = f32[8,100]{1,0:T(8,128)S(1)} copy-done((f32[8,100]{1,0:T(8,128)S(1)}, f32[8,100]{1,0:T(8,128)}, u32[]{:S(2)}) %copy-start) | copy-done | bytes 3224
  32.2 0.6 %copy.9 = f32[8,100]{1,0:T(8,128)} copy(f32[8,100]{1,0:T(8,128)S(1)} %copy-done) | data formatting | bytes 6400
  32.8 1.4 %copy.10 = f32[4,3,1024]{2,0,1:T(4,128)} copy(f32[4,3,1024]{2,0,1:T(4,128)} %bitcast.10) | data formatting | bytes 98304
Async XLA Ops:
  31.5 0.7 %copy-start = (f32[8,100]{1,0:T(8,128)S(1)}, f32[8,100]{1,0:T(8,128)}, u32[]{:S(2)}) copy-start(f32[8,100]{1,0:T(8,128)} %get-tuple-element.8) | copy-start | bytes 9604

commit v3 on v2

--- a/solution.py
+++ b/solution.py
@@ -101,8 +101,8 @@
     nt, ns, own_t, own_s,
     index_ref, label_ref, pool_ref, dual_ref, support_ref,
     residual_ref, grad_ref,
-    tbuf, dbuf, kbuf, srep, sroot, tlev, amp, ang, ksum, wexp, accl, accc, pred, flat,
-    plane_send, plane_recv, part_send, part_recv, dual_send, dual_recv, k_send, k_recv,
+    tbuf, hbuf, dbuf, kbuf, srep, sroot, tlev, amp, ang, ksum, wexp, accl, accc, pred, flat,
+    plane_send, plane_recv, sup_send, sup_recv, hot_send, hot_recv, part_send, part_recv, dual_send, dual_recv, k_send, k_recv,
 ):
     ti = lax.axis_index("tgt")
     si = lax.axis_index("sup")
@@ -146,53 +146,79 @@
     for r in range(own_t):
         label = jnp.where(row == r, label_ref[r], label)
     own_onehot = jnp.where(label == lane, 1.0, 0.0).astype(jnp.float32)
-    tbuf[ti, images] = own_onehot
+    hbuf[ti] = own_onehot
     dbuf[si] = dual_ref[...]
 
     pl.semaphore_wait(barrier, ndev - 1)
 
-    def chunk(owner, gl):
-        first = gl * CHANNELS * PACK
-        last = images + 1 if gl == groups_own - 1 else first + CHANNELS * PACK
-        return tbuf.at[owner, pl.ds(first, last - first)]
-
-    def plane_copy(source_chip, gl, way, target_chip):
-        part = chunk(source_chip * 2 + core, gl)
-        return pltpu.make_async_remote_copy(
-            src_ref=part,
-            dst_ref=part,
-            send_sem=plane_send.at[way, source_chip, gl],
-            recv_sem=plane_recv.at[source_chip, gl],
-            device_id=(target_chip * 2 + core, si),
-            device_id_type=MESH,
-        )
-
-    def part_copy(p, gl, side):
-        part = chunk(p * 2 + side, gl)
-        return pltpu.make_async_remote_copy(
-            src_ref=part,
-            dst_ref=part,
-            send_sem=part_send.at[p, gl],
-            recv_sem=part_recv.at[p, gl],
+    size = images // ns
+
+    def order(n):
+        both = jnp.minimum(chip, chips - 1 - chip)
+        h = (n + 1) // 2
+        two_sided = jnp.where(n % 2 == 1, chip - h, chip + h)
+        far = n - both
+        one_sided = jnp.where(chip <= chips - 1 - chip, chip + far, chip - far)
+        return jnp.where(n <= 2 * both, two_sided, one_sided)
+
+    def piece_copy(owner, j, send_sem, recv_sem, device):
+        piece = tbuf.at[owner, pl.ds(j * size, size)]
+        return pltpu.make_async_remote_copy(
+            src_ref=piece,
+            dst_ref=piece,
+            send_sem=send_sem,
+            recv_sem=recv_sem,
+            device_id=device,
+            device_id_type=MESH,
+        )
+
+    def plane_copy(source, target):
+        return piece_copy(
+            source * 2 + core, si, plane_send.at[target], plane_recv.at[source],
+            (target * 2 + core, si),
+        )
+
+    def sup_copy(p, j, s):
+        return piece_copy(p * 2 + core, j, sup_send.at[p, s], sup_recv.at[p, j], (ti, s))
+
+    def part_copy(p, j, side):
+        return piece_copy(
+            p * 2 + side, j, part_send.at[p, j], part_recv.at[p, j], (chip * 2 + 1 - core, si)
+        )
+
+    def hot_copy(t):
+        return pltpu.make_async_remote_copy(
+            src_ref=hbuf.at[ti],
+            dst_ref=hbuf.at[ti],
+            send_sem=hot_send,
+            recv_sem=hot_recv,
+            device_id=(t, si),
+            device_id_type=MESH,
+        )
+
+    def hot_all():
+        return pltpu.make_async_remote_copy(
+            src_ref=hbuf.at[pl.ds(0, nt - 1)],
+            dst_ref=hbuf.at[pl.ds(0, nt - 1)],
+            send_sem=hot_send,
+            recv_sem=hot_recv,
             device_id=(chip * 2 + 1 - core, si),
             device_id_type=MESH,
         )
 
-    def handle(h, gl):
-        for way in range(2):
-            step = 1 - 2 * way
-            source = chip - step * h
-            onward = chip + step
-
-            @pl.when((source >= 0) & (source < chips))
-            def _():
-                plane_copy(source, gl, way, source).wait_recv()
-
-                @pl.when((onward >= 0) & (onward < chips))
-                def _():
-                    plane_copy(source, gl, way, onward).start()
-
-                part_copy(source, gl, core).start()
+    def spread_own_piece(m):
+        p = order(m)
+        plane_copy(p, p).wait_recv()
+        for step in range(1, ns):
+            sup_copy(p, si, lax.rem(si + step, ns)).start()
+        part_copy(p, si, core).start()
+
+    def collect_pieces(m):
+        p = order(m)
+        for step in range(1, ns):
+            j = lax.rem(si + step, ns)
+            sup_copy(p, j, j).wait_recv()
+            part_copy(p, j, core).start()
 
     def dual_copy(s):
         return pltpu.make_async_remote_copy(
@@ -235,15 +261,16 @@
             device_id_type=MESH,
         )
 
-    for gl in range(groups_own):
-        for way in range(2):
-            onward = chip + 1 - 2 * way
-
-            @pl.when((onward >= 0) & (onward < chips))
+    for h in range(1, chips):
+        for target in (chip - h, chip + h):
+            @pl.when((target >= 0) & (target < chips))
             def _():
-                plane_copy(chip, gl, way, onward).start()
-
-        part_copy(chip, gl, core).start()
+                plane_copy(chip, target).start()
+
+    for j in range(ns):
+        part_copy(chip, j, core).start()
+    for t in range(nt):
+        pl.when(ti != t)(lambda t=t: hot_copy(t).start())
 
     def send_dual(step, carry):
         dual_copy(lax.rem(si + step, ns)).start()
@@ -307,26 +334,20 @@
         total = (mapped[0] + mapped[1]) + (mapped[2] + mapped[3])
         ksum[:, pl.ds(g, 1), :] = jnp.sum(total, axis=1, keepdims=True)
 
-    def order(n):
-        both = jnp.minimum(chip, chips - 1 - chip)
-        h = (n + 1) // 2
-        two_sided = jnp.where(n % 2 == 1, chip - h, chip + h)
-        far = n - both
-        one_sided = jnp.where(chip <= chips - 1 - chip, chip + far, chip - far)
-        return jnp.where(n <= 2 * both, two_sided, one_sided)
-
     def visit(slot, carry):
         n = slot // (2 * groups_own)
         at = slot % (2 * groups_own)
         gl = at % groups_own
         p = order(n)
-        for later in range(1, groups_own):
-            pl.when((n > 0) & (at == later))(functools.partial(handle, n, later))
-        pl.when((n + 1 < chips) & (at == 2 * groups_own - 1))(functools.partial(handle, n + 1, 0))
-        for which in range(groups_own):
-            @pl.when(at == groups_own + which)
-            def _():
-                part_copy(p, which, 1 - core).wait_recv()
+        per = 2 * groups_own
+        for m in range(1, chips):
+            pl.when(slot == 2 * m + 1)(functools.partial(spread_own_piece, m))
+            pl.when(slot == (per if m == 1 else per * m - 1))(functools.partial(collect_pieces, m))
+
+        @pl.when(at == groups_own)
+        def _():
+            for j in range(ns):
+                part_copy(p, j, 1 - core).wait_recv()
 
         side = jnp.where(at < groups_own, core, 1 - core)
         group_forward(p * 2 + side, gl)
@@ -360,7 +381,8 @@
     gram = lax.dot_general(
         own_duals, duals, nt_dims, precision=HIGH, preferred_element_type=jnp.float32
     )
-    onehot = tbuf[:, images].reshape(targets, LANES)[:, :CLASSES]
+    hot_all().wait_recv()
+    onehot = hbuf[...].reshape(targets, LANES)[:, :CLASSES]
     offset = lax.dot_general(
         own_duals, onehot, nt_dims, precision=HIGH, preferred_element_type=jnp.float32
     )
@@ -433,18 +455,17 @@
     pred[...] = jnp.dot(columns.T, duals, precision=HIGH, preferred_element_type=jnp.float32)
     residual_ref[...] = pred[pl.ds(ti * own_t, own_t), :] - own_onehot[:own_t, :CLASSES]
 
-    for gl in range(groups_own):
-        for way in range(2):
-            onward = chip + 1 - 2 * way
-            for h in range(chips):
-                source = chip - (1 - 2 * way) * h
-
-                @pl.when((source >= 0) & (source < chips) & (onward >= 0) & (onward < chips))
-                def _():
-                    plane_copy(source, gl, way, onward).wait_send()
-
-        for p in range(chips):
-            part_copy(p, gl, core).wait_send()
+    for p in range(chips):
+        @pl.when(chip != p)
+        def _():
+            plane_copy(chip, p).wait_send()
+            for step in range(1, ns):
+                sup_copy(p, si, lax.rem(si + step, ns)).wait_send()
+
+        for j in range(ns):
+            part_copy(p, j, core).wait_send()
+
+    hot_all().wait_send()
 
     def drain_dual(step, carry):
         dual_copy(lax.rem(si + step, ns)).wait_send()
@@ -476,7 +497,8 @@
         in_specs=[smem, smem, vmem, vmem, vmem],
         out_specs=(vmem, vmem),
         scratch_shapes=[
-            pltpu.VMEM((nt, images + 1) + tile, f32),
+            pltpu.VMEM((nt, images) + tile, f32),
+            pltpu.VMEM((nt,) + tile, f32),
             pltpu.VMEM((ns,) + dual_weights.shape, f32),
             pltpu.VMEM((ndev, own_s, nt * own_t), f32),
             pltpu.VMEM((CHANNELS, PACK, own_s) + tile, f32),
@@ -490,10 +512,14 @@
             pltpu.VMEM((CHANNELS, PACK, own_s) + tile, f32),
             pltpu.VMEM((nt * own_t, CLASSES), f32),
             pltpu.VMEM((own_s,) + tile, f32),
-            dma((2, chips, own_t // PACK)),
-            dma((chips, own_t // PACK)),
-            dma((chips, own_t // PACK)),
-            dma((chips, own_t // PACK)),
+            dma((chips,)),
+            dma((chips,)),
+            dma((chips, ns)),
+            dma((chips, ns)),
+            dma,
+            dma,
+            dma((chips, ns)),
+            dma((chips, ns)),
             dma((ns,)),
             dma((ns,)),
             dma,

time: 34.4 us -> 39.1 us (1.14)
  Pallas kernels: 30.9 us -> 35.5 us
    pallas_call x1, Pallas kernels: 30.9 us -> 35.5 us  [shards(): pl.pallas_call(functools.partial(kernel, nt, ns, own_t, own_s), out_shape...]
where the time goes in v3:
time: 39.1 us; the launch traced here: 38.8 us
  Pallas kernels  35.5 us (91%)
  local copies, waits for them, and re-layouts  2.68 us (7%)
  between operations  0.65 us (2%)
    pallas_call x1, Pallas kernels, shards(): pl.pallas_call(functools.partial(kernel, nt, ns, own_t, own_s), out_shape...  35.5 us
    unnamed x4, local copies, waits for them, and re-layouts  2.68 us

profile of v3, /device:TPU:0, one launch (start us, length us, event | category | flops | bytes accessed | tf_op | source)
XLA Modules:
  0.0 38.8 jit_solution(10387036556642507612)
XLA Ops:
  0.6 35.5 %shard_map.68 = (f32[8,100]{1,0:T(8,128)}, f32[3,8,4,128]{3,2,1,0:T(4,128)}) custom-call(s32[8]{0:T(128)} %index_ref.1, s32[8]{0:T(128)} %label_ref.1, f32[3,8,8,8,128]{4,3,2,1,0:T(8,128)} %bitcast.9, f32[32,100]{1,0:T(8,128)} %dual_ref.1, f32[3,8,4,128]{3,2,1,0:T(4,128)} %bitcast.11), custom_call_target="tpu_custom_call" | custom-call | tf_op jit(solution)/shard_map/pallas_call | solution.py:491
  36.1 0.0 copy-start
  36.2 0.7 %copy-done = f32[8,100]{1,0:T(8,128)S(1)} copy-done((f32[8,100]{1,0:T(8,128)S(1)}, f32[8,100]{1,0:T(8,128)}, u32[]{:S(2)}) %copy-start) | copy-done | bytes 3224
  36.8 0.6 %copy.9 = f32[8,100]{1,0:T(8,128)} copy(f32[8,100]{1,0:T(8,128)S(1)} %copy-done) | data formatting | bytes 6400
  37.4 1.4 %copy.10 = f32[4,3,1024]{2,0,1:T(4,128)} copy(f32[4,3,1024]{2,0,1:T(4,128)} %bitcast.10) | data formatting | bytes 98304
Async XLA Ops:
  36.1 0.7 %copy-start = (f32[8,100]{1,0:T(8,128)S(1)}, f32[8,100]{1,0:T(8,128)}, u32[]{:S(2)}) copy-start(f32[8,100]{1,0:T(8,128)} %get-tuple-element.8) | copy-start | bytes 9604
